TPU v7x, 32 devices: a whole 2x2x4 slice. The times are simulated.
32 devices in a mesh: groups: 2 (over x), row: 16 (over z, y, core).
Axes of the slice: x: 2, y: 2, z: 4, core: 2. Of those that a mesh axis runs over, the one named last changes fastest.
Arguments:
- pair: bfloat16 [256, 128, 128], P(('groups', 'row')), parts along dimension 0, may hold values from -6 to 6
- single: bfloat16 [256, 384], P(('groups', 'row')), parts along dimension 0, may hold values from -6 to 6
- token_mask: int32 [256], P('groups'), parts along dimension 0, may hold values 0 or 1
- chain_index: int32 [256], P('groups'), parts along dimension 0, may hold values from 0 to 7, as said below
- residue_index: int32 [256], P('groups'), parts along dimension 0, may hold values from 0 to 166, as said below
- pair_gain: float32 [128], replicated, may hold values from 0.25 to 1.75
- pair_norm_offset: float32 [128], replicated, may hold values from -3 to 3
- w_swish_a: bfloat16 [128, 512], replicated, may hold values from -0.5 to 0.5
- w_swish_b: bfloat16 [128, 512], replicated, may hold values from -0.5 to 0.5
- w_trans_out: bfloat16 [512, 128], replicated, may hold values from -0.25 to 0.25
- w_pair_bias: bfloat16 [128, 16], replicated, may hold values from -0.5 to 0.5
- w_project: bfloat16 [384, 1536], replicated, may hold values from -0.3125 to 0.3125
- w_out: bfloat16 [384, 384], replicated, may hold values from -0.3125 to 0.3125
- relative_position_bias: float32 [66, 16], replicated, may hold values from -6 to 300
Outputs:
- new_pair: bfloat16 [256, 128, 128], P(('groups', 'row')), parts along dimension 0
- single_update: bfloat16 [256, 384], P(('groups', 'row')), parts along dimension 0
There are 2 independent parts, one for each index of `groups`. A program takes and returns all parts, laid end to end along the dimension named above; an argument that names none is the same for every part. Nothing has to cross between parts.
Inputs may be any that keep to these rules, and one draw needn't show every extreme that they name: `chain_index`: chain numbers never fall along the tokens, start at 0, and every chain 0 to 7 holds one token or more. `residue_index`: within a chain each token's residue number is one more than the previous token's.
All inputs are finite; a program needn't handle non-finite values.
Results may differ from a plain program's by a relative error of at most 0.014.
Values may be sent and summed in bfloat16 or wider, within the bound.
A program may use at most 64 MiB of HBM per device.

v0:
```python
import functools
import math

import jax
import jax.numpy as jnp
from jax import lax
from jax.experimental import pallas as pl
from jax.experimental.pallas import tpu as pltpu
from jax.sharding import PartitionSpec as P

HEADS = 16
HEAD_DIM = 24
RELMAX = 32
BINS = 66
CLASSES = 80
ROWS_AT_ONCE = 512
GRANT = 24 * 1024 * 1024

epsilon = 1e-05
F32 = jnp.float32
BF16 = jnp.bfloat16


def layer_norm(value_rows):
    middle = jnp.mean(value_rows, axis=-1, keepdims=True)
    centred = value_rows - middle
    spread = jnp.mean(centred * centred, axis=-1, keepdims=True)
    return centred * lax.rsqrt(spread + epsilon)


def dot(a, b):
    return jnp.dot(a, b, preferred_element_type=F32)


def dot_nt(a, b):
    return lax.dot_general(a, b, (((1,), (1,)), ((), ())), preferred_element_type=F32)


def other(me, step, devices):
    return step + (step - me + devices) // devices


def own_columns(local, width):
    place = lax.broadcasted_iota(jnp.int32, (local, HEADS, width), 2) - HEAD_DIM * (
        lax.broadcasted_iota(jnp.int32, (local, HEADS, width), 1)
    )
    return (place >= 0) & (place < HEAD_DIM)


def kernel(
    devices,
    pair_hbm,
    single_hbm,
    chain_hbm,
    res_hbm,
    gain_hbm,
    offset_hbm,
    wa_hbm,
    wb_hbm,
    wt_hbm,
    wpb_hbm,
    wp_hbm,
    table_hbm,
    new_pair_ref,
    bias,
    keys_ref,
    spread_ref,
    gates_ref,
    wv_ref,
    pair,
    gathered,
    chain,
    res,
    gain,
    offset,
    wa,
    wb,
    wt,
    wpb,
    wp,
    table,
    load_sem,
    send_sem,
    recv_sem,
):
    me = lax.axis_index("row")
    local, tokens, channels = pair.shape
    width = gathered.shape[2]

    loads = [
        pltpu.make_async_copy(src, dst, load_sem.at[i])
        for i, (src, dst) in enumerate(
            (
                (single_hbm, gathered.at[me]),
                (chain_hbm, chain),
                (res_hbm, res),
                (table_hbm, table),
                (pair_hbm, pair),
                (gain_hbm, gain),
                (offset_hbm, offset),
                (wa_hbm, wa),
                (wb_hbm, wb),
                (wt_hbm, wt),
                (wpb_hbm, wpb),
                (wp_hbm, wp),
            )
        )
    ]
    barrier = pltpu.get_barrier_semaphore()

    def greet(step, carry):
        pl.semaphore_signal(
            barrier,
            inc=1,
            device_id={"row": other(me, step, devices)},
            device_id_type=pl.DeviceIdType.MESH,
        )
        return carry

    for load in loads[:1]:
        load.start()
    lax.fori_loop(0, devices - 1, greet, 0, unroll=devices <= 16)
    for load in loads[1:]:
        load.start()

    def copy_between(sender, receiver):
        return pltpu.make_async_remote_copy(
            src_ref=gathered.at[sender],
            dst_ref=gathered.at[sender],
            send_sem=send_sem.at[receiver],
            recv_sem=recv_sem.at[sender],
            device_id={"row": receiver},
            device_id_type=pl.DeviceIdType.MESH,
        )

    loads[0].wait()
    at_once = max(1, ROWS_AT_ONCE // tokens)
    span = min(tokens, ROWS_AT_ONCE)
    pieces = tokens // span

    def transition(chunk, half_wa, wpb_t):
        row = pl.ds((chunk // pieces) * at_once, at_once)
        start = (chunk % pieces) * span
        if not isinstance(start, int):
            start = pl.multiple_of(start, span)
        col = pl.ds(start, span)
        x = pair[row, col, :].reshape(at_once * span, channels).astype(F32)
        normed = (layer_norm(x) * gain[...] + offset[...]).astype(BF16)
        h = dot(normed, half_wa)
        second = dot(normed, wb[...])
        hidden = ((h + h * jnp.tanh(h)) * second).astype(BF16)
        updated = (x + dot(hidden, wt[...])).astype(BF16)
        new_pair_ref[row, col, :] = updated.reshape(at_once, span, channels)
        bias_input = layer_norm(updated.astype(F32)).astype(BF16)
        head_rows = dot_nt(wpb_t, bias_input).astype(BF16).astype(F32)
        for i in range(at_once):
            at = ((chunk // pieces) * at_once + i, slice(None), col)
            bias[at] = bias[at] + head_rows[:, i * span : (i + 1) * span]

    chunks = (local // at_once) * pieces
    def pair_work():
        for load in loads[1:4]:
            load.wait()
        at = lax.broadcasted_iota(jnp.int32, (local, tokens), 1)
        own_at = lax.broadcasted_iota(jnp.int32, (local, tokens), 0) + me * local
        res_all = res[...].astype(F32)
        chain_all = chain[...].astype(F32)
        here = at == own_at
        own_res = jnp.sum(jnp.where(here, res_all, 0.0), axis=1, keepdims=True)
        own_chain = jnp.sum(jnp.where(here, chain_all, 0.0), axis=1, keepdims=True)
        bins = jnp.where(
            own_chain == chain_all,
            jnp.clip(own_res - res_all + RELMAX, 0.0, 2.0 * RELMAX),
            2.0 * RELMAX + 1.0,
        ).astype(jnp.int32)
        table_t = jnp.concatenate(
            [table[...], jnp.zeros((HEADS, CLASSES - BINS), F32)], axis=1
        )
        high = table_t.astype(BF16)
        rest = table_t - high.astype(F32)
        middle = rest.astype(BF16)
        low = (rest - middle.astype(F32)).astype(BF16)
        classes = lax.broadcasted_iota(jnp.int32, (CLASSES, tokens), 0)
        for r in range(local):
            hot = jnp.where(classes == bins[r : r + 1, :], 1.0, 0.0).astype(BF16)
            bias[r] = dot(high, hot) + (dot(middle, hot) + dot(low, hot))

        for load in loads[4:11]:
            load.wait()
        half_wa = wa[...] * BF16(0.5)
        wpb_t = wpb[...]

        if chunks <= 8:
            for chunk in range(chunks):
                transition(chunk, half_wa, wpb_t)
        else:

            def body(chunk, carry):
                transition(chunk, half_wa, wpb_t)
                return carry

            lax.fori_loop(0, chunks, body, 0)

    ahead = me < 2
    pl.when(ahead)(pair_work)
    pl.semaphore_wait(barrier, devices - 1)

    def send(step, carry):
        copy_between(me, other(me, step, devices)).start()
        return carry

    lax.fori_loop(0, devices - 1, send, 0, unroll=devices <= 16)
    pl.when(jnp.logical_not(ahead))(pair_work)

    loads[11].wait()
    own = layer_norm(gathered[me].astype(F32)).astype(BF16)
    queries = dot(own, wp[:, :width]).astype(BF16).astype(F32)
    gates = dot(own, wp[:, 3 * width :]).astype(BF16).astype(F32)
    gates_ref[...] = gates
    wv_ref[...] = wp[:, 2 * width : 3 * width]
    mine = own_columns(local, width)
    spread_queries = jnp.where(mine, queries[:, None, :], 0.0)
    spread_queries = spread_queries.reshape(local * HEADS, width).astype(BF16)
    spread_queries = dot_nt(spread_queries, wp[:, width : 2 * width]) * (
        1.0 / math.sqrt(HEAD_DIM)
    )
    spread_ref[...] = spread_queries.astype(BF16)

    def arrive(step, carry):
        copy_between(other(me, step, devices), me).wait_recv()
        return carry

    def leave(step, carry):
        copy_between(me, other(me, step, devices)).wait_send()
        return carry

    lax.fori_loop(0, devices - 1, arrive, 0, unroll=devices <= 16)
    normed = layer_norm(gathered[...].astype(F32).reshape(tokens, width)).astype(BF16)
    keys_ref[...] = normed
    lax.fori_loop(0, devices - 1, leave, 0, unroll=devices <= 16)


def attention(
    new_pair_from,
    bias,
    keys,
    spread_queries,
    gates,
    wv,
    mask,
    wo,
    new_pair_ref,
    update_ref,
    out_sem,
):
    local, width = gates.shape
    tokens = keys.shape[0]
    out = pltpu.make_async_copy(new_pair_from, new_pair_ref, out_sem)
    out.start()
    values = dot(keys[...], wv[...]).astype(BF16)
    mine = own_columns(local, width)
    scores = dot_nt(spread_queries[...], keys[...]) + bias[...].reshape(local * HEADS, tokens)
    scores = jnp.where(mask[...] > 0, scores, -1000000000.0)
    expons = jnp.exp(scores - jnp.max(scores, axis=1, keepdims=True))
    totals = jnp.sum(expons, axis=1, keepdims=True)
    attended = dot(expons.astype(BF16), values) / totals
    attended = jnp.sum(
        jnp.where(mine, attended.reshape(local, HEADS, width), 0.0), axis=1
    )
    gated = (jax.nn.sigmoid(gates[...]) * attended).astype(BF16)
    update_ref[...] = dot(gated, wo[...]).astype(BF16)
    out.wait()


def on_device(
    devices,
    pair,
    single,
    token_mask,
    chain_index,
    residue_index,
    pair_gain,
    pair_norm_offset,
    w_swish_a,
    w_swish_b,
    w_trans_out,
    w_pair_bias,
    w_project,
    w_out,
    relative_position_bias,
):
    def line(vector):
        return vector.reshape(1, vector.shape[0])

    operands = (
        pair,
        single,
        line(chain_index),
        line(residue_index),
        line(pair_gain),
        line(pair_norm_offset),
        w_swish_a,
        w_swish_b,
        w_trans_out,
        w_pair_bias.T,
        w_project,
        relative_position_bias.T,
    )
    local, tokens, _ = pair.shape
    width = single.shape[1]
    anywhere = pl.BlockSpec(memory_space=pl.ANY)
    vmem = pl.BlockSpec(memory_space=pltpu.VMEM)
    held = [pltpu.VMEM(pair.shape, pair.dtype), pltpu.VMEM((devices,) + single.shape, single.dtype)]
    held += [pltpu.VMEM(x.shape, x.dtype) for x in operands[2:]]
    operands = [pltpu.with_memory_space_constraint(x, pltpu.HBM) for x in operands]
    handed = pl.pallas_call(
        functools.partial(kernel, devices),
        out_shape=(
            jax.ShapeDtypeStruct(pair.shape, BF16),
            jax.ShapeDtypeStruct((local, HEADS, tokens), F32),
            jax.ShapeDtypeStruct((tokens, width), BF16),
            jax.ShapeDtypeStruct((local * HEADS, width), BF16),
            jax.ShapeDtypeStruct((local, width), F32),
            jax.ShapeDtypeStruct((width, width), BF16),
        ),
        in_specs=[anywhere] * len(operands),
        out_specs=(vmem,) * 6,
        scratch_shapes=held
        + [
            pltpu.SemaphoreType.DMA((len(operands),)),
            pltpu.SemaphoreType.DMA((devices,)),
            pltpu.SemaphoreType.DMA((devices,)),
        ],
        compiler_params=pltpu.CompilerParams(
            collective_id=0, has_side_effects=True, vmem_limit_bytes=GRANT
        ),
        name="pair_tail",
    )(*operands)
    return pl.pallas_call(
        attention,
        out_shape=(
            jax.ShapeDtypeStruct(pair.shape, BF16),
            jax.ShapeDtypeStruct(single.shape, BF16),
        ),
        in_specs=[anywhere] + [vmem] * 7,
        out_specs=(anywhere, vmem),
        scratch_shapes=[pltpu.SemaphoreType.DMA],
        compiler_params=pltpu.CompilerParams(vmem_limit_bytes=GRANT),
        name="single_attention",
    )(*handed, line(token_mask), w_out)


def solution(mesh):
    rows = P(("groups", "row"))
    return jax.shard_map(
        functools.partial(on_device, mesh.shape["row"]),
        mesh=mesh,
        in_specs=(rows, rows) + (P("groups"),) * 3 + (P(),) * 9,
        out_specs=(rows, rows),
        check_vma=False,
    )
```

profile of v0, /device:TPU:0, one launch (start us, length us, event | category | flops | bytes accessed | tf_op | source)
XLA Modules:
  0.0 11.5 jit_solution(6933377935851495975)
XLA Ops:
  0.6 0.0 copy-start
  0.6 0.0 copy-start.1
  0.7 9.4 %pair_tail.1 = (bf16[8,128,128]{2,1,0:T(8,128)(2,1)S(1)}, f32[8,16,128]{2,1,0:T(8,128)S(1)}, bf16[128,384]{1,0:T(8,128)(2,1)S(1)}, bf16[128,384]{1,0:T(8,128)(2,...) custom-call(bf16[8,128,128]{2,1,0:T(8,128)(2,1)} %pair_hbm.1, bf16[8,384]{1,0:T(8,128)(2,1)} %single_hbm.1, ...), custom_call_target="tpu_custom_call" | custom-call | tf_op jit(solution)/shard_map/pair_tail/pallas_call | solution.py:316
  10.1 0.0 copy-done
  10.1 0.0 copy-done.1
  10.1 1.4 %single_attention.1 = (bf16[8,128,128]{2,1,0:T(8,128)(2,1)}, bf16[8,384]{1,0:T(8,128)(2,1)}) custom-call(bf16[8,128,128]{2,1,0:T(8,128)(2,1)S(1)} %get-tuple-element.8.new_pair_from, f32[8,16,128]{2,1,0:T(8,128)S(1)} %get-tuple-element.9.bias, bf16[128,384]{1,0:T(8,128)(2,1)S(1)} %get-tuple-element.10.keys, ...), custom_call_target="tpu_custom_call" | custom-call | tf_op jit(solution)/shard_map/single_attention/pallas_call | solution.py:339
Async XLA Ops:
  0.6 9.4 %copy-start = (bf16[384,384]{1,0:T(8,128)(2,1)S(1)}, bf16[384,384]{1,0:T(8,128)(2,1)}, u32[]{:S(2)}) copy-start(bf16[384,384]{1,0:T(8,128)(2,1)} %wo.1) | copy-start | bytes 884740
  0.6 9.4 %copy-start.1 = (s32[128]{0:T(128)S(1)}, s32[128]{0:T(128)}, u32[]{:S(2)}) copy-start(s32[128]{0:T(128)} %param.16) | copy-start | bytes 1540
where the time goes:
time: 11.6 us; the launch traced here: 11.5 us
  Pallas kernels  10.8 us (93%)
  between operations  0.68 us (6%)
    pallas_call x1, Pallas kernels, on_device(): pl.pallas_call(functools.partial(kernel, devices), out_shape=(jax.ShapeDt...  9.41 us
    pallas_call x1, Pallas kernels, on_device(): pl.pallas_call(attention, out_shape=(jax.ShapeDtypeStruct(pair.shape, BF1...  1.39 us

commit v1 on v0

--- a/solution.py
+++ b/solution.py
@@ -14,6 +14,7 @@
 BINS = 66
 CLASSES = 80
 ROWS_AT_ONCE = 512
+LANES = 128
 GRANT = 24 * 1024 * 1024
 
 epsilon = 1e-05
@@ -41,8 +42,8 @@
 
 
 def own_columns(local, width):
-    place = lax.broadcasted_iota(jnp.int32, (local, HEADS, width), 2) - HEAD_DIM * (
-        lax.broadcasted_iota(jnp.int32, (local, HEADS, width), 1)
+    place = lax.broadcasted_iota(jnp.int32, (HEADS, local, width), 2) - HEAD_DIM * (
+        lax.broadcasted_iota(jnp.int32, (HEADS, local, width), 0)
     )
     return (place >= 0) & (place < HEAD_DIM)
 
@@ -62,13 +63,14 @@
     wp_hbm,
     table_hbm,
     new_pair_ref,
-    bias,
+    bias_ref,
     keys_ref,
     spread_ref,
     gates_ref,
     wv_ref,
     pair,
     gathered,
+    bias,
     chain,
     res,
     gain,
@@ -127,8 +129,8 @@
         return pltpu.make_async_remote_copy(
             src_ref=gathered.at[sender],
             dst_ref=gathered.at[sender],
-            send_sem=send_sem.at[receiver],
-            recv_sem=recv_sem.at[sender],
+            send_sem=send_sem,
+            recv_sem=recv_sem,
             device_id={"row": receiver},
             device_id_type=pl.DeviceIdType.MESH,
         )
@@ -216,28 +218,31 @@
     own = layer_norm(gathered[me].astype(F32)).astype(BF16)
     queries = dot(own, wp[:, :width]).astype(BF16).astype(F32)
     gates = dot(own, wp[:, 3 * width :]).astype(BF16).astype(F32)
-    gates_ref[...] = gates
+    gates_ref[...] = jax.nn.sigmoid(gates)
     wv_ref[...] = wp[:, 2 * width : 3 * width]
     mine = own_columns(local, width)
-    spread_queries = jnp.where(mine, queries[:, None, :], 0.0)
-    spread_queries = spread_queries.reshape(local * HEADS, width).astype(BF16)
+    spread_queries = jnp.where(mine, queries[None, :, :], 0.0)
+    spread_queries = spread_queries.reshape(HEADS * local, width).astype(BF16)
     spread_queries = dot_nt(spread_queries, wp[:, width : 2 * width]) * (
         1.0 / math.sqrt(HEAD_DIM)
     )
     spread_ref[...] = spread_queries.astype(BF16)
-
-    def arrive(step, carry):
-        copy_between(other(me, step, devices), me).wait_recv()
-        return carry
-
-    def leave(step, carry):
-        copy_between(me, other(me, step, devices)).wait_send()
-        return carry
-
-    lax.fori_loop(0, devices - 1, arrive, 0, unroll=devices <= 16)
+    for i in range(local):
+        bias_ref[:, i, :] = bias[i]
+
+    partners = gathered.at[pl.ds(0, devices - 1)]
+    everyone = pltpu.make_async_remote_copy(
+        src_ref=partners,
+        dst_ref=partners,
+        send_sem=send_sem,
+        recv_sem=recv_sem,
+        device_id={"row": other(me, 0, devices)},
+        device_id_type=pl.DeviceIdType.MESH,
+    )
+    everyone.wait_send()
+    everyone.wait_recv()
     normed = layer_norm(gathered[...].astype(F32).reshape(tokens, width)).astype(BF16)
     keys_ref[...] = normed
-    lax.fori_loop(0, devices - 1, leave, 0, unroll=devices <= 16)
 
 
 def attention(
@@ -251,25 +256,40 @@
     wo,
     new_pair_ref,
     update_ref,
+    update,
     out_sem,
+    update_sem,
 ):
     local, width = gates.shape
     tokens = keys.shape[0]
     out = pltpu.make_async_copy(new_pair_from, new_pair_ref, out_sem)
     out.start()
+    scores = dot_nt(spread_queries[...], keys[...])
+    scores = scores + bias[...].reshape(HEADS * local, tokens)
+    scores = jnp.where(mask[...] > 0, scores, -1000000000.0)
+    expons = jnp.exp(scores - jnp.max(scores, axis=1, keepdims=True)).astype(BF16)
     values = dot(keys[...], wv[...]).astype(BF16)
-    mine = own_columns(local, width)
-    scores = dot_nt(spread_queries[...], keys[...]) + bias[...].reshape(local * HEADS, tokens)
-    scores = jnp.where(mask[...] > 0, scores, -1000000000.0)
-    expons = jnp.exp(scores - jnp.max(scores, axis=1, keepdims=True))
-    totals = jnp.sum(expons, axis=1, keepdims=True)
-    attended = dot(expons.astype(BF16), values) / totals
-    attended = jnp.sum(
-        jnp.where(mine, attended.reshape(local, HEADS, width), 0.0), axis=1
-    )
-    gated = (jax.nn.sigmoid(gates[...]) * attended).astype(BF16)
-    update_ref[...] = dot(gated, wo[...]).astype(BF16)
-    out.wait()
+    values = jnp.concatenate([values, jnp.ones((tokens, LANES), BF16)], axis=1)
+    spread = dot(expons, values)
+    shares = 1.0 / spread[:, width:]
+    column = lax.broadcasted_iota(jnp.int32, (local, LANES), 1)
+    pieces = []
+    for first in range(0, width, LANES):
+        piece = jnp.zeros((local, LANES), F32)
+        for head in range(HEADS):
+            begin, end = head * HEAD_DIM - first, (head + 1) * HEAD_DIM - first
+            if begin < LANES and end > 0:
+                rows = slice(head * local, (head + 1) * local)
+                part = spread[rows, first : first + LANES] * shares[rows]
+                piece = jnp.where((column >= begin) & (column < end), part, piece)
+        pieces.append(piece)
+    attended = jnp.concatenate(pieces, axis=1)
+    gated = (gates[...] * attended).astype(BF16)
+    update[...] = dot(gated, wo[...]).astype(BF16)
+    done = pltpu.make_async_copy(update, update_ref, update_sem)
+    done.start()
+    done.wait()
+    pltpu.make_async_copy(new_pair_from, new_pair_ref, out_sem).wait()
 
 
 def on_device(
@@ -310,14 +330,18 @@
     width = single.shape[1]
     anywhere = pl.BlockSpec(memory_space=pl.ANY)
     vmem = pl.BlockSpec(memory_space=pltpu.VMEM)
-    held = [pltpu.VMEM(pair.shape, pair.dtype), pltpu.VMEM((devices,) + single.shape, single.dtype)]
+    held = [
+        pltpu.VMEM(pair.shape, pair.dtype),
+        pltpu.VMEM((devices,) + single.shape, single.dtype),
+        pltpu.VMEM((local, HEADS, tokens), F32),
+    ]
     held += [pltpu.VMEM(x.shape, x.dtype) for x in operands[2:]]
     operands = [pltpu.with_memory_space_constraint(x, pltpu.HBM) for x in operands]
     handed = pl.pallas_call(
         functools.partial(kernel, devices),
         out_shape=(
             jax.ShapeDtypeStruct(pair.shape, BF16),
-            jax.ShapeDtypeStruct((local, HEADS, tokens), F32),
+            jax.ShapeDtypeStruct((HEADS, local, tokens), F32),
             jax.ShapeDtypeStruct((tokens, width), BF16),
             jax.ShapeDtypeStruct((local * HEADS, width), BF16),
             jax.ShapeDtypeStruct((local, width), F32),
@@ -328,8 +352,8 @@
         scratch_shapes=held
         + [
             pltpu.SemaphoreType.DMA((len(operands),)),
-            pltpu.SemaphoreType.DMA((devices,)),
-            pltpu.SemaphoreType.DMA((devices,)),
+            pltpu.SemaphoreType.DMA,
+            pltpu.SemaphoreType.DMA,
         ],
         compiler_params=pltpu.CompilerParams(
             collective_id=0, has_side_effects=True, vmem_limit_bytes=GRANT
@@ -343,8 +367,8 @@
             jax.ShapeDtypeStruct(single.shape, BF16),
         ),
         in_specs=[anywhere] + [vmem] * 7,
-        out_specs=(anywhere, vmem),
-        scratch_shapes=[pltpu.SemaphoreType.DMA],
+        out_specs=(anywhere, anywhere),
+        scratch_shapes=[pltpu.VMEM(single.shape, BF16), pltpu.SemaphoreType.DMA, pltpu.SemaphoreType.DMA],
         compiler_params=pltpu.CompilerParams(vmem_limit_bytes=GRANT),
         name="single_attention",
     )(*handed, line(token_mask), w_out)

time: 11.6 us -> 11.1 us (0.957)
  Pallas kernels: 10.8 us -> 10.3 us
    pallas_call x1, Pallas kernels: 9.41 us -> 9.1 us  [on_device(): pl.pallas_call(functools.partial(kernel, devices), out_shape=(jax.ShapeDt...]
    pallas_call x1, Pallas kernels: 1.39 us -> 1.19 us  [on_device(): pl.pallas_call(attention, out_shape=(jax.ShapeDtypeStruct(pair.shape, BF1...]
where the time goes in v1:
time: 11.1 us; the launch traced here: 11 us
  Pallas kernels  10.3 us (93%)
  between operations  0.68 us (6%)
    pallas_call x1, Pallas kernels, on_device(): pl.pallas_call(functools.partial(kernel, devices), out_shape=(jax.ShapeDt...  9.1 us
    pallas_call x1, Pallas kernels, on_device(): pl.pallas_call(attention, out_shape=(jax.ShapeDtypeStruct(pair.shape, BF1...  1.19 us

profile of v1, /device:TPU:0, one launch (start us, length us, event | category | flops | bytes accessed | tf_op | source)
XLA Modules:
  0.0 11.0 jit_solution(5493102841788636559)
XLA Ops:
  0.6 0.0 copy-start
  0.6 0.0 copy-start.1
  0.7 9.1 %pair_tail.1 = (bf16[8,128,128]{2,1,0:T(8,128)(2,1)S(1)}, f32[16,8,128]{2,1,0:T(8,128)S(1)}, bf16[128,384]{1,0:T(8,128)(2,1)S(1)}, bf16[128,384]{1,0:T(8,128)(2,...) custom-call(bf16[8,128,128]{2,1,0:T(8,128)(2,1)} %pair_hbm.1, bf16[8,384]{1,0:T(8,128)(2,1)} %single_hbm.1, ...), custom_call_target="tpu_custom_call" | custom-call | tf_op jit(solution)/shard_map/pair_tail/pallas_call | solution.py:340
  9.8 0.0 copy-done
  9.8 0.0 copy-done.1
  9.8 1.2 %single_attention.1 = (bf16[8,128,128]{2,1,0:T(8,128)(2,1)}, bf16[8,384]{1,0:T(8,128)(2,1)}) custom-call(bf16[8,128,128]{2,1,0:T(8,128)(2,1)S(1)} %get-tuple-element.8.new_pair_from, f32[16,8,128]{2,1,0:T(8,128)S(1)} %get-tuple-element.9.bias, bf16[128,384]{1,0:T(8,128)(2,1)S(1)} %get-tuple-element.10.keys, ...), custom_call_target="tpu_custom_call" | custom-call | tf_op jit(solution)/shard_map/single_attention/pallas_call | solution.py:363
Async XLA Ops:
  0.6 9.1 %copy-start = (bf16[384,384]{1,0:T(8,128)(2,1)S(1)}, bf16[384,384]{1,0:T(8,128)(2,1)}, u32[]{:S(2)}) copy-start(bf16[384,384]{1,0:T(8,128)(2,1)} %wo.1) | copy-start | bytes 884740
  0.6 9.1 %copy-start.1 = (s32[128]{0:T(128)S(1)}, s32[128]{0:T(128)}, u32[]{:S(2)}) copy-start(s32[128]{0:T(128)} %param.16) | copy-start | bytes 1540

commit v2 on v1

--- a/solution.py
+++ b/solution.py
@@ -15,6 +15,7 @@
 CLASSES = 80
 ROWS_AT_ONCE = 512
 LANES = 128
+FRINGE = 2
 GRANT = 24 * 1024 * 1024
 
 epsilon = 1e-05
@@ -84,6 +85,7 @@
     load_sem,
     send_sem,
     recv_sem,
+    late_sem,
 ):
     me = lax.axis_index("row")
     local, tokens, channels = pair.shape
@@ -110,30 +112,60 @@
     ]
     barrier = pltpu.get_barrier_semaphore()
 
-    def greet(step, carry):
+    last = devices - FRINGE
+    is_early, is_late = me < FRINGE, me >= last
+    is_middle = jnp.logical_not(jnp.logical_or(is_early, is_late))
+
+    def repeat(count, act):
+        def body(step, carry):
+            act(step)
+            return carry
+
+        lax.fori_loop(0, count, body, 0, unroll=devices <= 16)
+
+    def greet(receiver):
         pl.semaphore_signal(
             barrier,
             inc=1,
-            device_id={"row": other(me, step, devices)},
-            device_id_type=pl.DeviceIdType.MESH,
-        )
-        return carry
-
-    for load in loads[:1]:
-        load.start()
-    lax.fori_loop(0, devices - 1, greet, 0, unroll=devices <= 16)
-    for load in loads[1:]:
-        load.start()
-
-    def copy_between(sender, receiver):
-        return pltpu.make_async_remote_copy(
-            src_ref=gathered.at[sender],
-            dst_ref=gathered.at[sender],
-            send_sem=send_sem,
-            recv_sem=recv_sem,
             device_id={"row": receiver},
             device_id_type=pl.DeviceIdType.MESH,
         )
+
+    def send(receiver, arrival):
+        pltpu.make_async_remote_copy(
+            src_ref=gathered.at[me],
+            dst_ref=gathered.at[me],
+            send_sem=send_sem,
+            recv_sem=arrival,
+            device_id={"row": receiver},
+            device_id_type=pl.DeviceIdType.MESH,
+        ).start()
+
+    def blocks(count, arrival):
+        some = gathered.at[pl.ds(0, count)]
+        return pltpu.make_async_remote_copy(
+            src_ref=some,
+            dst_ref=some,
+            send_sem=send_sem,
+            recv_sem=arrival,
+            device_id={"row": other(me, 0, devices)},
+            device_id_type=pl.DeviceIdType.MESH,
+        )
+
+    loads[0].start()
+
+    @pl.when(is_late)
+    def _():
+        for receiver in range(FRINGE):
+            greet(receiver)
+        repeat(FRINGE - 1, lambda step: greet(last + other(me - last, step, FRINGE)))
+
+    @pl.when(jnp.logical_not(is_late))
+    def _():
+        repeat(devices - 1, lambda step: greet(other(me, step, devices)))
+
+    for load in loads[1:]:
+        load.start()
 
     loads[0].wait()
     at_once = max(1, ROWS_AT_ONCE // tokens)
@@ -160,7 +192,13 @@
             bias[at] = bias[at] + head_rows[:, i * span : (i + 1) * span]
 
     chunks = (local // at_once) * pieces
-    def pair_work():
+    def answer():
+        @pl.when(is_middle)
+        def _():
+            blocks(FRINGE, late_sem).wait_recv()
+            repeat(FRINGE, lambda step: send(last + step, recv_sem))
+
+    def pair_work(answer=lambda: None):
         for load in loads[1:4]:
             load.wait()
         at = lax.broadcasted_iota(jnp.int32, (local, tokens), 1)
@@ -194,6 +232,8 @@
 
         if chunks <= 8:
             for chunk in range(chunks):
+                if chunk == chunks - 1:
+                    answer()
                 transition(chunk, half_wa, wpb_t)
         else:
 
@@ -202,17 +242,30 @@
                 return carry
 
             lax.fori_loop(0, chunks, body, 0)
-
-    ahead = me < 2
-    pl.when(ahead)(pair_work)
-    pl.semaphore_wait(barrier, devices - 1)
-
-    def send(step, carry):
-        copy_between(me, other(me, step, devices)).start()
-        return carry
-
-    lax.fori_loop(0, devices - 1, send, 0, unroll=devices <= 16)
-    pl.when(jnp.logical_not(ahead))(pair_work)
+            answer()
+
+    pl.when(is_early)(pair_work)
+
+    @pl.when(is_late)
+    def _():
+        pl.semaphore_wait(barrier, devices - 1)
+        for receiver in range(FRINGE):
+            send(receiver, late_sem)
+        repeat(FRINGE - 1, lambda step: send(last + other(me - last, step, FRINGE), late_sem))
+        repeat(last - FRINGE, lambda step: send(FRINGE + step, late_sem))
+
+    @pl.when(is_middle)
+    def _():
+        pl.semaphore_wait(barrier, last - 1)
+        repeat(last - 1, lambda step: send(other(me, step, devices), recv_sem))
+
+    @pl.when(is_early)
+    def _():
+        pl.semaphore_wait(barrier, devices - 1)
+        repeat(FRINGE, lambda step: send(last + step, recv_sem))
+        repeat(last - 1, lambda step: send(other(me, step, devices), recv_sem))
+
+    pl.when(jnp.logical_not(is_early))(lambda: pair_work(answer))
 
     loads[11].wait()
     own = layer_norm(gathered[me].astype(F32)).astype(BF16)
@@ -230,17 +283,21 @@
     for i in range(local):
         bias_ref[:, i, :] = bias[i]
 
-    partners = gathered.at[pl.ds(0, devices - 1)]
-    everyone = pltpu.make_async_remote_copy(
-        src_ref=partners,
-        dst_ref=partners,
-        send_sem=send_sem,
-        recv_sem=recv_sem,
-        device_id={"row": other(me, 0, devices)},
-        device_id_type=pl.DeviceIdType.MESH,
-    )
-    everyone.wait_send()
-    everyone.wait_recv()
+    @pl.when(is_middle)
+    def _():
+        blocks(last - 1, recv_sem).wait_recv()
+
+    @pl.when(is_late)
+    def _():
+        blocks(FRINGE - 1, late_sem).wait_recv()
+        blocks(last, recv_sem).wait_recv()
+
+    @pl.when(is_early)
+    def _():
+        blocks(last - 1, recv_sem).wait_recv()
+        blocks(FRINGE, late_sem).wait_recv()
+
+    blocks(devices - 1, recv_sem).wait_send()
     normed = layer_norm(gathered[...].astype(F32).reshape(tokens, width)).astype(BF16)
     keys_ref[...] = normed
 
@@ -354,6 +411,7 @@
             pltpu.SemaphoreType.DMA((len(operands),)),
             pltpu.SemaphoreType.DMA,
             pltpu.SemaphoreType.DMA,
+            pltpu.SemaphoreType.DMA,
         ],
         compiler_params=pltpu.CompilerParams(
             collective_id=0, has_side_effects=True, vmem_limit_bytes=GRANT

time: 11.1 us -> 10.9 us (0.982)
  Pallas kernels: 10.3 us -> 10 us
    pallas_call x1, Pallas kernels: 9.1 us -> 8.86 us  [on_device(): pl.pallas_call(functools.partial(kernel, devices), out_shape=(jax.ShapeDt...]
where the time goes in v2:
time: 10.9 us; the launch traced here: 10.7 us
  Pallas kernels  10 us (92%)
  between operations  0.68 us (6%)
    pallas_call x1, Pallas kernels, on_device(): pl.pallas_call(functools.partial(kernel, devices), out_shape=(jax.ShapeDt...  8.86 us
    pallas_call x1, Pallas kernels, on_device(): pl.pallas_call(attention, out_shape=(jax.ShapeDtypeStruct(pair.shape, BF1...  1.19 us

profile of v2, /device:TPU:0, one launch (start us, length us, event | category | flops | bytes accessed | tf_op | source)
XLA Modules:
  0.0 10.7 jit_solution(3928418808424232918)
XLA Ops:
  0.6 0.0 copy-start
  0.6 0.0 copy-start.1
  0.7 8.9 %pair_tail.1 = (bf16[8,128,128]{2,1,0:T(8,128)(2,1)S(1)}, f32[16,8,128]{2,1,0:T(8,128)S(1)}, bf16[128,384]{1,0:T(8,128)(2,1)S(1)}, bf16[128,384]{1,0:T(8,128)(2,...) custom-call(bf16[8,128,128]{2,1,0:T(8,128)(2,1)} %pair_hbm.1, bf16[8,384]{1,0:T(8,128)(2,1)} %single_hbm.1, ...), custom_call_target="tpu_custom_call" | custom-call | tf_op jit(solution)/shard_map/pair_tail/pallas_call | solution.py:397
  9.5 0.0 copy-done
  9.5 0.0 copy-done.1
  9.5 1.2 %single_attention.1 = (bf16[8,128,128]{2,1,0:T(8,128)(2,1)}, bf16[8,384]{1,0:T(8,128)(2,1)}) custom-call(bf16[8,128,128]{2,1,0:T(8,128)(2,1)S(1)} %get-tuple-element.8.new_pair_from, f32[16,8,128]{2,1,0:T(8,128)S(1)} %get-tuple-element.9.bias, bf16[128,384]{1,0:T(8,128)(2,1)S(1)} %get-tuple-element.10.keys, ...), custom_call_target="tpu_custom_call" | custom-call | tf_op jit(solution)/shard_map/single_attention/pallas_call | solution.py:421
Async XLA Ops:
  0.6 8.9 %copy-start = (bf16[384,384]{1,0:T(8,128)(2,1)S(1)}, bf16[384,384]{1,0:T(8,128)(2,1)}, u32[]{:S(2)}) copy-start(bf16[384,384]{1,0:T(8,128)(2,1)} %wo.1) | copy-start | bytes 884740
  0.6 8.9 %copy-start.1 = (s32[128]{0:T(128)S(1)}, s32[128]{0:T(128)}, u32[]{:S(2)}) copy-start(s32[128]{0:T(128)} %param.16) | copy-start | bytes 1540

commit v3 on v2

--- a/solution.py
+++ b/solution.py
@@ -70,7 +70,7 @@
     gates_ref,
     wv_ref,
     pair,
-    gathered,
+    single,
     bias,
     chain,
     res,
@@ -89,13 +89,14 @@
 ):
     me = lax.axis_index("row")
     local, tokens, channels = pair.shape
-    width = gathered.shape[2]
+    width = single.shape[1]
+    mine_at = pl.ds(pl.multiple_of(me * local, local), local)
 
     loads = [
         pltpu.make_async_copy(src, dst, load_sem.at[i])
         for i, (src, dst) in enumerate(
             (
-                (single_hbm, gathered.at[me]),
+                (single_hbm, single),
                 (chain_hbm, chain),
                 (res_hbm, res),
                 (table_hbm, table),
@@ -133,8 +134,8 @@
 
     def send(receiver, arrival):
         pltpu.make_async_remote_copy(
-            src_ref=gathered.at[me],
-            dst_ref=gathered.at[me],
+            src_ref=keys_ref.at[mine_at],
+            dst_ref=keys_ref.at[mine_at],
             send_sem=send_sem,
             recv_sem=arrival,
             device_id={"row": receiver},
@@ -142,7 +143,7 @@
         ).start()
 
     def blocks(count, arrival):
-        some = gathered.at[pl.ds(0, count)]
+        some = keys_ref.at[pl.ds(0, count * local)]
         return pltpu.make_async_remote_copy(
             src_ref=some,
             dst_ref=some,
@@ -168,6 +169,7 @@
         load.start()
 
     loads[0].wait()
+    keys_ref[mine_at, :] = layer_norm(single[...].astype(F32)).astype(BF16)
     at_once = max(1, ROWS_AT_ONCE // tokens)
     span = min(tokens, ROWS_AT_ONCE)
     pieces = tokens // span
@@ -268,7 +270,7 @@
     pl.when(jnp.logical_not(is_early))(lambda: pair_work(answer))
 
     loads[11].wait()
-    own = layer_norm(gathered[me].astype(F32)).astype(BF16)
+    own = layer_norm(single[...].astype(F32)).astype(BF16)
     queries = dot(own, wp[:, :width]).astype(BF16).astype(F32)
     gates = dot(own, wp[:, 3 * width :]).astype(BF16).astype(F32)
     gates_ref[...] = jax.nn.sigmoid(gates)
@@ -298,8 +300,6 @@
         blocks(FRINGE, late_sem).wait_recv()
 
     blocks(devices - 1, recv_sem).wait_send()
-    normed = layer_norm(gathered[...].astype(F32).reshape(tokens, width)).astype(BF16)
-    keys_ref[...] = normed
 
 
 def attention(
@@ -389,7 +389,7 @@
     vmem = pl.BlockSpec(memory_space=pltpu.VMEM)
     held = [
         pltpu.VMEM(pair.shape, pair.dtype),
-        pltpu.VMEM((devices,) + single.shape, single.dtype),
+        pltpu.VMEM(single.shape, single.dtype),
         pltpu.VMEM((local, HEADS, tokens), F32),
     ]
     held += [pltpu.VMEM(x.shape, x.dtype) for x in operands[2:]]

time: 10.9 us -> 10.7 us (0.982)
  Pallas kernels: 10 us -> 9.88 us
    pallas_call x1, Pallas kernels: 8.86 us -> 8.7 us  [on_device(): pl.pallas_call(functools.partial(kernel, devices), out_shape=(jax.ShapeDt...]
where the time goes in v3:
time: 10.7 us; the launch traced here: 10.6 us
  Pallas kernels  9.88 us (92%)
  between operations  0.68 us (6%)
    pallas_call x1, Pallas kernels, on_device(): pl.pallas_call(functools.partial(kernel, devices), out_shape=(jax.ShapeDt...  8.7 us
    pallas_call x1, Pallas kernels, on_device(): pl.pallas_call(attention, out_shape=(jax.ShapeDtypeStruct(pair.shape, BF1...  1.19 us

profile of v3, /device:TPU:0, one launch (start us, length us, event | category | flops | bytes accessed | tf_op | source)
XLA Modules:
  0.0 10.6 jit_solution(14774674049226958157)
XLA Ops:
  0.6 0.0 copy-start
  0.6 0.0 copy-start.1
  0.7 8.7 %pair_tail.1 = (bf16[8,128,128]{2,1,0:T(8,128)(2,1)S(1)}, f32[16,8,128]{2,1,0:T(8,128)S(1)}, bf16[128,384]{1,0:T(8,128)(2,1)S(1)}, bf16[128,384]{1,0:T(8,128)(2,...) custom-call(bf16[8,128,128]{2,1,0:T(8,128)(2,1)} %pair_hbm.1, bf16[8,384]{1,0:T(8,128)(2,1)} %single_hbm.1, ...), custom_call_target="tpu_custom_call" | custom-call | tf_op jit(solution)/shard_map/pair_tail/pallas_call | solution.py:397
  9.4 0.0 copy-done
  9.4 0.0 copy-done.1
  9.4 1.2 %single_attention.1 = (bf16[8,128,128]{2,1,0:T(8,128)(2,1)}, bf16[8,384]{1,0:T(8,128)(2,1)}) custom-call(bf16[8,128,128]{2,1,0:T(8,128)(2,1)S(1)} %get-tuple-element.8.new_pair_from, f32[16,8,128]{2,1,0:T(8,128)S(1)} %get-tuple-element.9.bias, bf16[128,384]{1,0:T(8,128)(2,1)S(1)} %get-tuple-element.10.keys, ...), custom_call_target="tpu_custom_call" | custom-call | tf_op jit(solution)/shard_map/single_attention/pallas_call | solution.py:421
Async XLA Ops:
  0.6 8.7 %copy-start = (bf16[384,384]{1,0:T(8,128)(2,1)S(1)}, bf16[384,384]{1,0:T(8,128)(2,1)}, u32[]{:S(2)}) copy-start(bf16[384,384]{1,0:T(8,128)(2,1)} %wo.1) | copy-start | bytes 884740
  0.6 8.7 %copy-start.1 = (s32[128]{0:T(128)S(1)}, s32[128]{0:T(128)}, u32[]{:S(2)}) copy-start(s32[128]{0:T(128)} %param.16) | copy-start | bytes 1540

commit v4 on v3

--- a/solution.py
+++ b/solution.py
@@ -66,9 +66,8 @@
     new_pair_ref,
     bias_ref,
     keys_ref,
-    spread_ref,
+    stack_ref,
     gates_ref,
-    wv_ref,
     pair,
     single,
     bias,
@@ -93,7 +92,7 @@
     mine_at = pl.ds(pl.multiple_of(me * local, local), local)
 
     loads = [
-        pltpu.make_async_copy(src, dst, load_sem.at[i])
+        pltpu.make_async_copy(src, dst, load_sem.at[min(i, 1) + i // 11])
         for i, (src, dst) in enumerate(
             (
                 (single_hbm, single),
@@ -201,7 +200,7 @@
             repeat(FRINGE, lambda step: send(last + step, recv_sem))
 
     def pair_work(answer=lambda: None):
-        for load in loads[1:4]:
+        for load in loads[1:11]:
             load.wait()
         at = lax.broadcasted_iota(jnp.int32, (local, tokens), 1)
         own_at = lax.broadcasted_iota(jnp.int32, (local, tokens), 0) + me * local
@@ -227,8 +226,6 @@
             hot = jnp.where(classes == bins[r : r + 1, :], 1.0, 0.0).astype(BF16)
             bias[r] = dot(high, hot) + (dot(middle, hot) + dot(low, hot))
 
-        for load in loads[4:11]:
-            load.wait()
         half_wa = wa[...] * BF16(0.5)
         wpb_t = wpb[...]
 
@@ -251,15 +248,18 @@
     @pl.when(is_late)
     def _():
         pl.semaphore_wait(barrier, devices - 1)
-        for receiver in range(FRINGE):
-            send(receiver, late_sem)
+        send(0, late_sem)
+        repeat(4, lambda step: send(FRINGE + step, late_sem))
+        send(1, late_sem)
+        repeat(last - FRINGE - 4, lambda step: send(FRINGE + 4 + step, late_sem))
         repeat(FRINGE - 1, lambda step: send(last + other(me - last, step, FRINGE), late_sem))
-        repeat(last - FRINGE, lambda step: send(FRINGE + step, late_sem))
 
     @pl.when(is_middle)
     def _():
         pl.semaphore_wait(barrier, last - 1)
-        repeat(last - 1, lambda step: send(other(me, step, devices), recv_sem))
+        send(0, recv_sem)
+        send(1, recv_sem)
+        repeat(last - 1 - FRINGE, lambda step: send(other(me, last - 2 - step, devices), recv_sem))
 
     @pl.when(is_early)
     def _():
@@ -274,14 +274,15 @@
     queries = dot(own, wp[:, :width]).astype(BF16).astype(F32)
     gates = dot(own, wp[:, 3 * width :]).astype(BF16).astype(F32)
     gates_ref[...] = jax.nn.sigmoid(gates)
-    wv_ref[...] = wp[:, 2 * width : 3 * width]
+    values_t = wp[:, 2 * width : 3 * width].astype(F32).T.astype(BF16)
+    stack_ref[HEADS * local :, :] = values_t
     mine = own_columns(local, width)
     spread_queries = jnp.where(mine, queries[None, :, :], 0.0)
     spread_queries = spread_queries.reshape(HEADS * local, width).astype(BF16)
     spread_queries = dot_nt(spread_queries, wp[:, width : 2 * width]) * (
         1.0 / math.sqrt(HEAD_DIM)
     )
-    spread_ref[...] = spread_queries.astype(BF16)
+    stack_ref[: HEADS * local, :] = spread_queries.astype(BF16)
     for i in range(local):
         bias_ref[:, i, :] = bias[i]
 
@@ -306,9 +307,8 @@
     new_pair_from,
     bias,
     keys,
-    spread_queries,
+    stack,
     gates,
-    wv,
     mask,
     wo,
     new_pair_ref,
@@ -321,24 +321,25 @@
     tokens = keys.shape[0]
     out = pltpu.make_async_copy(new_pair_from, new_pair_ref, out_sem)
     out.start()
-    scores = dot_nt(spread_queries[...], keys[...])
-    scores = scores + bias[...].reshape(HEADS * local, tokens)
+    both = dot_nt(stack[...], keys[...])
+    scores = both[: HEADS * local] + bias[...].reshape(HEADS * local, tokens)
     scores = jnp.where(mask[...] > 0, scores, -1000000000.0)
     expons = jnp.exp(scores - jnp.max(scores, axis=1, keepdims=True)).astype(BF16)
-    values = dot(keys[...], wv[...]).astype(BF16)
-    values = jnp.concatenate([values, jnp.ones((tokens, LANES), BF16)], axis=1)
-    spread = dot(expons, values)
-    shares = 1.0 / spread[:, width:]
+    values_t = both[HEADS * local :].astype(BF16)
+    ones = jnp.ones((LANES, tokens), BF16)
     column = lax.broadcasted_iota(jnp.int32, (local, LANES), 1)
     pieces = []
     for first in range(0, width, LANES):
-        piece = jnp.zeros((local, LANES), F32)
-        for head in range(HEADS):
-            begin, end = head * HEAD_DIM - first, (head + 1) * HEAD_DIM - first
-            if begin < LANES and end > 0:
-                rows = slice(head * local, (head + 1) * local)
-                part = spread[rows, first : first + LANES] * shares[rows]
-                piece = jnp.where((column >= begin) & (column < end), part, piece)
+        heads = range(first // HEAD_DIM, -(-(first + LANES) // HEAD_DIM))
+        spread = dot_nt(
+            expons[heads[0] * local : (heads[-1] + 1) * local],
+            jnp.concatenate([values_t[first : first + LANES], ones], axis=0),
+        )
+        spread = spread[:, :LANES] / spread[:, LANES:]
+        piece = spread[:local]
+        for at, head in enumerate(heads[1:], 1):
+            part = spread[at * local : (at + 1) * local]
+            piece = jnp.where(column >= head * HEAD_DIM - first, part, piece)
         pieces.append(piece)
     attended = jnp.concatenate(pieces, axis=1)
     gated = (gates[...] * attended).astype(BF16)
@@ -400,15 +401,14 @@
             jax.ShapeDtypeStruct(pair.shape, BF16),
             jax.ShapeDtypeStruct((HEADS, local, tokens), F32),
             jax.ShapeDtypeStruct((tokens, width), BF16),
-            jax.ShapeDtypeStruct((local * HEADS, width), BF16),
+            jax.ShapeDtypeStruct((HEADS * local + width, width), BF16),
             jax.ShapeDtypeStruct((local, width), F32),
-            jax.ShapeDtypeStruct((width, width), BF16),
         ),
         in_specs=[anywhere] * len(operands),
-        out_specs=(vmem,) * 6,
+        out_specs=(vmem,) * 5,
         scratch_shapes=held
         + [
-            pltpu.SemaphoreType.DMA((len(operands),)),
+            pltpu.SemaphoreType.DMA((3,)),
             pltpu.SemaphoreType.DMA,
             pltpu.SemaphoreType.DMA,
             pltpu.SemaphoreType.DMA,
@@ -424,7 +424,7 @@
             jax.ShapeDtypeStruct(pair.shape, BF16),
             jax.ShapeDtypeStruct(single.shape, BF16),
         ),
-        in_specs=[anywhere] + [vmem] * 7,
+        in_specs=[anywhere] + [vmem] * 6,
         out_specs=(anywhere, anywhere),
         scratch_shapes=[pltpu.VMEM(single.shape, BF16), pltpu.SemaphoreType.DMA, pltpu.SemaphoreType.DMA],
         compiler_params=pltpu.CompilerParams(vmem_limit_bytes=GRANT),

time: 10.7 us -> 10.6 us (level)
  no operation moved by 1% of the time
where the time goes in v4:
time: 10.6 us; the launch traced here: 10.5 us
  Pallas kernels  9.78 us (92%)
  between operations  0.68 us (6%)
    pallas_call x1, Pallas kernels, on_device(): pl.pallas_call(functools.partial(kernel, devices), out_shape=(jax.ShapeDt...  8.62 us
    pallas_call x1, Pallas kernels, on_device(): pl.pallas_call(attention, out_shape=(jax.ShapeDtypeStruct(pair.shape, BF1...  1.17 us

profile of v4, /device:TPU:0, one launch (start us, length us, event | category | flops | bytes accessed | tf_op | source)
XLA Modules:
  0.0 10.5 jit_solution(16809958517247257207)
XLA Ops:
  0.6 0.0 copy-start
  0.6 0.0 copy-start.1
  0.7 8.6 %pair_tail.1 = (bf16[8,128,128]{2,1,0:T(8,128)(2,1)S(1)}, f32[16,8,128]{2,1,0:T(8,128)S(1)}, bf16[128,384]{1,0:T(8,128)(2,1)S(1)}, bf16[512,384]{1,0:T(8,128)(2,1)S(1)}, f32[8,384]{1,0:T(8,128)S(1)}) custom-call(bf16[8,128,128]{2,1,0:T(8,128)(2,1)} %pair_hbm.1, bf16[8,384]{1,0:T(8,128)(2,1)} %single_hbm.1, s32[1,128]{1,0:T(1,128)} %bitcast.10, ...), custom_call_target="tpu_custom_call" | custom-call | tf_op jit(solution)/shard_map/pair_tail/pallas_call | solution.py:398
  9.3 0.0 copy-done
  9.3 0.0 copy-done.1
  9.3 1.2 %single_attention.1 = (bf16[8,128,128]{2,1,0:T(8,128)(2,1)}, bf16[8,384]{1,0:T(8,128)(2,1)}) custom-call(bf16[8,128,128]{2,1,0:T(8,128)(2,1)S(1)} %get-tuple-element.7.new_pair_from, f32[16,8,128]{2,1,0:T(8,128)S(1)} %get-tuple-element.8.bias, bf16[128,384]{1,0:T(8,128)(2,1)S(1)} %get-tuple-element.9.keys, bf16[512,384]{1,0:T(8,128)(2,1)S(1)} %get-tuple-element.10.stack, ...), custom_call_target="tpu_custom_call" | custom-call | tf_op jit(solution)/shard_map/single_attention/pallas_call | solution.py:421
Async XLA Ops:
  0.6 8.6 %copy-start = (bf16[384,384]{1,0:T(8,128)(2,1)S(1)}, bf16[384,384]{1,0:T(8,128)(2,1)}, u32[]{:S(2)}) copy-start(bf16[384,384]{1,0:T(8,128)(2,1)} %wo.1) | copy-start | bytes 884740
  0.6 8.6 %copy-start.1 = (s32[128]{0:T(128)S(1)}, s32[128]{0:T(128)}, u32[]{:S(2)}) copy-start(s32[128]{0:T(128)} %param.16) | copy-start | bytes 1540

commit v5 on v4

--- a/solution.py
+++ b/solution.py
@@ -335,11 +335,12 @@
             expons[heads[0] * local : (heads[-1] + 1) * local],
             jnp.concatenate([values_t[first : first + LANES], ones], axis=0),
         )
-        spread = spread[:, :LANES] / spread[:, LANES:]
-        piece = spread[:local]
+        own = spread[:local]
         for at, head in enumerate(heads[1:], 1):
             part = spread[at * local : (at + 1) * local]
-            piece = jnp.where(column >= head * HEAD_DIM - first, part, piece)
+            reached = jnp.concatenate([column, column], axis=1) >= head * HEAD_DIM - first
+            own = jnp.where(reached, part, own)
+        piece = own[:, :LANES] / own[:, LANES:]
         pieces.append(piece)
     attended = jnp.concatenate(pieces, axis=1)
     gated = (gates[...] * attended).astype(BF16)

time: 10.6 us -> 10.6 us (level)
  no operation moved by 1% of the time
where the time goes in v5:
time: 10.6 us; the launch traced here: 10.5 us
  Pallas kernels  9.78 us (92%)
  between operations  0.68 us (6%)
    pallas_call x1, Pallas kernels, on_device(): pl.pallas_call(functools.partial(kernel, devices), out_shape=(jax.ShapeDt...  8.62 us
    pallas_call x1, Pallas kernels, on_device(): pl.pallas_call(attention, out_shape=(jax.ShapeDtypeStruct(pair.shape, BF1...  1.17 us

profile of v5, /device:TPU:0, one launch (start us, length us, event | category | flops | bytes accessed | tf_op | source)
XLA Modules:
  0.0 10.5 jit_solution(7490867995790313373)
XLA Ops:
  0.6 0.0 copy-start
  0.6 0.0 copy-start.1
  0.7 8.6 %pair_tail.1 = (bf16[8,128,128]{2,1,0:T(8,128)(2,1)S(1)}, f32[16,8,128]{2,1,0:T(8,128)S(1)}, bf16[128,384]{1,0:T(8,128)(2,1)S(1)}, bf16[512,384]{1,0:T(8,128)(2,1)S(1)}, f32[8,384]{1,0:T(8,128)S(1)}) custom-call(bf16[8,128,128]{2,1,0:T(8,128)(2,1)} %pair_hbm.1, bf16[8,384]{1,0:T(8,128)(2,1)} %single_hbm.1, s32[1,128]{1,0:T(1,128)} %bitcast.10, ...), custom_call_target="tpu_custom_call" | custom-call | tf_op jit(solution)/shard_map/pair_tail/pallas_call | solution.py:399
  9.3 0.0 copy-done
  9.3 0.0 copy-done.1
  9.3 1.2 %single_attention.1 = (bf16[8,128,128]{2,1,0:T(8,128)(2,1)}, bf16[8,384]{1,0:T(8,128)(2,1)}) custom-call(bf16[8,128,128]{2,1,0:T(8,128)(2,1)S(1)} %get-tuple-element.7.new_pair_from, f32[16,8,128]{2,1,0:T(8,128)S(1)} %get-tuple-element.8.bias, bf16[128,384]{1,0:T(8,128)(2,1)S(1)} %get-tuple-element.9.keys, bf16[512,384]{1,0:T(8,128)(2,1)S(1)} %get-tuple-element.10.stack, ...), custom_call_target="tpu_custom_call" | custom-call | tf_op jit(solution)/shard_map/single_attention/pallas_call | solution.py:422
Async XLA Ops:
  0.6 8.6 %copy-start = (bf16[384,384]{1,0:T(8,128)(2,1)S(1)}, bf16[384,384]{1,0:T(8,128)(2,1)}, u32[]{:S(2)}) copy-start(bf16[384,384]{1,0:T(8,128)(2,1)} %wo.1) | copy-start | bytes 884740
  0.6 8.6 %copy-start.1 = (s32[128]{0:T(128)S(1)}, s32[128]{0:T(128)}, u32[]{:S(2)}) copy-start(s32[128]{0:T(128)} %param.16) | copy-start | bytes 1540

commit v6 on v5

--- a/solution.py
+++ b/solution.py
@@ -15,6 +15,7 @@
 CLASSES = 80
 ROWS_AT_ONCE = 512
 LANES = 128
+LOG2E = 1.0 / math.log(2.0)
 FRINGE = 2
 GRANT = 24 * 1024 * 1024
 
@@ -280,11 +281,11 @@
     spread_queries = jnp.where(mine, queries[None, :, :], 0.0)
     spread_queries = spread_queries.reshape(HEADS * local, width).astype(BF16)
     spread_queries = dot_nt(spread_queries, wp[:, width : 2 * width]) * (
-        1.0 / math.sqrt(HEAD_DIM)
+        LOG2E / math.sqrt(HEAD_DIM)
     )
     stack_ref[: HEADS * local, :] = spread_queries.astype(BF16)
     for i in range(local):
-        bias_ref[:, i, :] = bias[i]
+        bias_ref[:, i, :] = bias[i] * LOG2E
 
     @pl.when(is_middle)
     def _():
@@ -323,8 +324,8 @@
     out.start()
     both = dot_nt(stack[...], keys[...])
     scores = both[: HEADS * local] + bias[...].reshape(HEADS * local, tokens)
-    scores = jnp.where(mask[...] > 0, scores, -1000000000.0)
-    expons = jnp.exp(scores - jnp.max(scores, axis=1, keepdims=True)).astype(BF16)
+    scores = jnp.where(mask[...] > 0, scores, -1000000000.0 * LOG2E)
+    expons = jnp.exp2(scores - jnp.max(scores, axis=1, keepdims=True)).astype(BF16)
     values_t = both[HEADS * local :].astype(BF16)
     ones = jnp.ones((LANES, tokens), BF16)
     column = lax.broadcasted_iota(jnp.int32, (local, LANES), 1)

time: 10.6 us -> 10.6 us (level)
  no operation moved by 1% of the time
where the time goes in v6:
time: 10.6 us; the launch traced here: 10.5 us
  Pallas kernels  9.78 us (92%)
  between operations  0.68 us (6%)
    pallas_call x1, Pallas kernels, on_device(): pl.pallas_call(functools.partial(kernel, devices), out_shape=(jax.ShapeDt...  8.62 us
    pallas_call x1, Pallas kernels, on_device(): pl.pallas_call(attention, out_shape=(jax.ShapeDtypeStruct(pair.shape, BF1...  1.17 us

profile of v6, /device:TPU:0, one launch (start us, length us, event | category | flops | bytes accessed | tf_op | source)
XLA Modules:
  0.0 10.5 jit_solution(14626420742205881321)
XLA Ops:
  0.6 0.0 copy-start
  0.6 0.0 copy-start.1
  0.7 8.6 %pair_tail.1 = (bf16[8,128,128]{2,1,0:T(8,128)(2,1)S(1)}, f32[16,8,128]{2,1,0:T(8,128)S(1)}, bf16[128,384]{1,0:T(8,128)(2,1)S(1)}, bf16[512,384]{1,0:T(8,128)(2,1)S(1)}, f32[8,384]{1,0:T(8,128)S(1)}) custom-call(bf16[8,128,128]{2,1,0:T(8,128)(2,1)} %pair_hbm.1, bf16[8,384]{1,0:T(8,128)(2,1)} %single_hbm.1, s32[1,128]{1,0:T(1,128)} %bitcast.10, ...), custom_call_target="tpu_custom_call" | custom-call | tf_op jit(solution)/shard_map/pair_tail/pallas_call | solution.py:400
  9.3 0.0 copy-done
  9.3 0.0 copy-done.1
  9.3 1.2 %single_attention.1 = (bf16[8,128,128]{2,1,0:T(8,128)(2,1)}, bf16[8,384]{1,0:T(8,128)(2,1)}) custom-call(bf16[8,128,128]{2,1,0:T(8,128)(2,1)S(1)} %get-tuple-element.7.new_pair_from, f32[16,8,128]{2,1,0:T(8,128)S(1)} %get-tuple-element.8.bias, bf16[128,384]{1,0:T(8,128)(2,1)S(1)} %get-tuple-element.9.keys, bf16[512,384]{1,0:T(8,128)(2,1)S(1)} %get-tuple-element.10.stack, ...), custom_call_target="tpu_custom_call" | custom-call | tf_op jit(solution)/shard_map/single_attention/pallas_call | solution.py:423
Async XLA Ops:
  0.6 8.6 %copy-start = (bf16[384,384]{1,0:T(8,128)(2,1)S(1)}, bf16[384,384]{1,0:T(8,128)(2,1)}, u32[]{:S(2)}) copy-start(bf16[384,384]{1,0:T(8,128)(2,1)} %wo.1) | copy-start | bytes 884740
  0.6 8.6 %copy-start.1 = (s32[128]{0:T(128)S(1)}, s32[128]{0:T(128)}, u32[]{:S(2)}) copy-start(s32[128]{0:T(128)} %param.16) | copy-start | bytes 1540

commit v7 on v5

--- a/solution.py
+++ b/solution.py
@@ -162,7 +162,8 @@
 
     @pl.when(jnp.logical_not(is_late))
     def _():
-        repeat(devices - 1, lambda step: greet(other(me, step, devices)))
+        repeat(devices - 1 - FRINGE, lambda step: greet(other(me, step + FRINGE, devices)))
+        repeat(FRINGE, lambda step: greet(other(me, step, devices)))
 
     for load in loads[1:]:
         load.start()

time: 10.6 us -> 10.6 us (level)
  no operation moved by 1% of the time
where the time goes in v7:
time: 10.6 us; the launch traced here: 10.5 us
  Pallas kernels  9.78 us (92%)
  between operations  0.68 us (6%)
    pallas_call x1, Pallas kernels, on_device(): pl.pallas_call(functools.partial(kernel, devices), out_shape=(jax.ShapeDt...  8.62 us
    pallas_call x1, Pallas kernels, on_device(): pl.pallas_call(attention, out_shape=(jax.ShapeDtypeStruct(pair.shape, BF1...  1.16 us

profile of v7, /device:TPU:0, one launch (start us, length us, event | category | flops | bytes accessed | tf_op | source)
XLA Modules:
  0.0 10.5 jit_solution(15040358997333938013)
XLA Ops:
  0.6 0.0 copy-start
  0.6 0.0 copy-start.1
  0.7 8.6 %pair_tail.1 = (bf16[8,128,128]{2,1,0:T(8,128)(2,1)S(1)}, f32[16,8,128]{2,1,0:T(8,128)S(1)}, bf16[128,384]{1,0:T(8,128)(2,1)S(1)}, bf16[512,384]{1,0:T(8,128)(2,1)S(1)}, f32[8,384]{1,0:T(8,128)S(1)}) custom-call(bf16[8,128,128]{2,1,0:T(8,128)(2,1)} %pair_hbm.1, bf16[8,384]{1,0:T(8,128)(2,1)} %single_hbm.1, s32[1,128]{1,0:T(1,128)} %bitcast.10, ...), custom_call_target="tpu_custom_call" | custom-call | tf_op jit(solution)/shard_map/pair_tail/pallas_call | solution.py:400
  9.3 0.0 copy-done
  9.3 0.0 copy-done.1
  9.3 1.2 %single_attention.1 = (bf16[8,128,128]{2,1,0:T(8,128)(2,1)}, bf16[8,384]{1,0:T(8,128)(2,1)}) custom-call(bf16[8,128,128]{2,1,0:T(8,128)(2,1)S(1)} %get-tuple-element.7.new_pair_from, f32[16,8,128]{2,1,0:T(8,128)S(1)} %get-tuple-element.8.bias, bf16[128,384]{1,0:T(8,128)(2,1)S(1)} %get-tuple-element.9.keys, bf16[512,384]{1,0:T(8,128)(2,1)S(1)} %get-tuple-element.10.stack, ...), custom_call_target="tpu_custom_call" | custom-call | tf_op jit(solution)/shard_map/single_attention/pallas_call | solution.py:423
Async XLA Ops:
  0.6 8.6 %copy-start = (bf16[384,384]{1,0:T(8,128)(2,1)S(1)}, bf16[384,384]{1,0:T(8,128)(2,1)}, u32[]{:S(2)}) copy-start(bf16[384,384]{1,0:T(8,128)(2,1)} %wo.1) | copy-start | bytes 884740
  0.6 8.6 %copy-start.1 = (s32[128]{0:T(128)S(1)}, s32[128]{0:T(128)}, u32[]{:S(2)}) copy-start(s32[128]{0:T(128)} %param.16) | copy-start | bytes 1540
